TPU v7x, 32 devices: a whole 2x2x4 slice. The times are simulated.
32 devices in a mesh: group: 4 (over y, x), ctx: 8 (over z, core).
Axes of the slice: x: 2, y: 2, z: 4, core: 2. Of those that a mesh axis runs over, the one named last changes fastest.
Arguments:
- hidden_in: bfloat16 [256, 4096], P(('group', 'ctx')), may hold values from -3 to 3
- queries: bfloat16 [256, 4096], P(('group', 'ctx')), may hold values from -120 to 120
- block_kv: bfloat16 [256, 2, 512], P(('group', 'ctx')), may hold values from -4 to 4
- cache: bfloat16 [8, 2, 4096, 512], P('group', None, 'ctx'), may hold values from -4 to 4
- lengths: int32 [8], P('group'), may hold values from 2 to 4096
- out_proj: bfloat16 [4096, 4096], P('ctx'), may hold values from -1.5 to 1.5
- norm_gain: float32 [4096], replicated, may hold values from 0.1 to 1.9
- expert_ids: int32 [256, 8], P(('group', 'ctx')), may hold values from 0 to 31, all different within a row; in each aligned block of 8 rows (0 to 7, 8 to 15, ...) at most 4 rows name the same one
- gate_weights: float32 [256, 8], P(('group', 'ctx')), may hold values from 0.05 to 1
- expert_gate: bfloat16 [32, 4096, 512], P(('group', 'ctx')), may hold values from -0.09375 to 0.09375
- expert_up: bfloat16 [32, 4096, 512], P(('group', 'ctx')), may hold values from -0.09375 to 0.09375
- expert_down: bfloat16 [32, 512, 4096], P(('group', 'ctx')), may hold values from -0.25 to 0.25
Outputs:
- attended: bfloat16 [256, 4096], P(('group', 'ctx'))
- layer_out: bfloat16 [256, 4096], P(('group', 'ctx'))
Inputs may be any that keep to these rules, and one draw needn't show every extreme that they name: `expert_ids`: each row names 8 different experts; among the rows of one device no expert is named more than 4 times. `lengths`: cache positions at and beyond a request's length hold no keys for it.
All inputs are finite; a program needn't handle non-finite values.
Results may differ from a plain program's by a relative error of at most 0.0054.
Values may be sent and summed in bfloat16 or wider, within the bound.
No kernel may reach another device: no remote copies, remote signals or barrier semaphores. Data moves between devices by JAX's collectives and lax.ppermute only.
A program may use at most 128 MiB of HBM per device.

v0:
```python
import jax
import jax.numpy as jnp
from jax import lax
from jax.sharding import PartitionSpec as P

HEAD_DIM = 128
BLOCK = 32


def body(
    hidden_in,
    queries,
    block_kv,
    cache,
    lengths,
    out_proj,
    norm_gain,
    expert_ids,
    gate_weights,
    expert_gate,
    expert_up,
    expert_down,
):
    ctx_size = lax.axis_size("ctx")
    group_count = lax.axis_size("group")
    ctx_index = lax.axis_index("ctx")
    tok_dev, model_width = hidden_in.shape
    requests, _, cache_dev, kv_width = cache.shape
    head_dim = HEAD_DIM
    block_len = BLOCK
    kv_heads = kv_width // head_dim
    num_heads = queries.shape[1] // head_dim
    group_size = num_heads // kv_heads
    heads_here = num_heads // ctx_size
    gathered = lax.all_gather(queries, "ctx", axis=0, tiled=True)
    query_blocks = gathered.reshape(requests, block_len, kv_heads, group_size, head_dim)
    cache_keys = cache[:, 0].reshape(requests, cache_dev, kv_heads, head_dim)
    cache_values = cache[:, 1].reshape(requests, cache_dev, kv_heads, head_dim)
    block_keys = block_kv[:, 0].reshape(tok_dev, kv_heads, head_dim)
    block_values = block_kv[:, 1].reshape(tok_dev, kv_heads, head_dim)
    score_scale = head_dim ** (-0.5)
    cache_scores = (
        jnp.einsum(
            "rbkgd,rckd->rkgbc", query_blocks, cache_keys, preferred_element_type=jnp.float32
        )
        * score_scale
    )
    block_scores = (
        jnp.einsum("rbkgd,tkd->rkgbt", query_blocks, block_keys, preferred_element_type=jnp.float32)
        * score_scale
    )
    scores = jnp.concatenate([cache_scores, block_scores], -1)
    position = ctx_index * cache_dev + jnp.arange(cache_dev, dtype=jnp.int32)
    cache_allowed = position[None, :] < lengths[:, None]
    key_owner = (ctx_index * tok_dev + jnp.arange(tok_dev, dtype=jnp.int32)) // block_len
    block_allowed = key_owner[None, :] == jnp.arange(requests, dtype=jnp.int32)[:, None]
    allowed = jnp.concatenate([cache_allowed, block_allowed], 1)[:, None, None, None, :]
    local_peak = jnp.max(jnp.where(allowed, scores, -jnp.inf), -1)
    maximum = lax.pmax(local_peak, "ctx")
    probs = jnp.where(allowed, jnp.exp(scores - maximum[..., None]), 0.0)
    denominator = jnp.sum(probs, -1).reshape(requests, num_heads, block_len)
    all_values = jnp.concatenate(
        [cache_values, jnp.broadcast_to(block_values[None], (requests,) + block_values.shape)], 1
    )
    numerator = jnp.einsum(
        "rkgbl,rlkd->rkgbd",
        probs.astype(jnp.bfloat16),
        all_values,
        preferred_element_type=jnp.float32,
    )
    numerator = numerator.reshape(requests, num_heads, block_len, head_dim)
    numerator, denominator = (
        lax.psum_scatter(numerator, "ctx", scatter_dimension=1, tiled=True),
        lax.psum_scatter(denominator, "ctx", scatter_dimension=1, tiled=True),
    )
    combined = (numerator / denominator[..., None]).astype(jnp.bfloat16)
    heads_out = combined.transpose(0, 2, 1, 3).reshape(requests * block_len, heads_here * head_dim)
    attention = lax.psum_scatter(
        jnp.dot(heads_out, out_proj, preferred_element_type=jnp.float32),
        "ctx",
        scatter_dimension=0,
        tiled=True,
    )
    residual = hidden_in.astype(jnp.float32) + attention
    mean_square = jnp.mean(residual * residual, -1, keepdims=True)
    normed = (residual * lax.rsqrt(mean_square + 1e-06) * norm_gain).astype(jnp.bfloat16)
    top_count = expert_ids.shape[1]
    exp_dev = expert_gate.shape[0]
    devices = group_count * ctx_size
    experts = exp_dev * devices
    capacity = max(2, (2 * tok_dev * top_count + experts - 1) // experts)
    flat_ids = expert_ids.reshape(-1)
    one_hot = (flat_ids[:, None] == jnp.arange(experts, dtype=jnp.int32)[None, :]).astype(jnp.int32)
    running_count = jnp.cumsum(one_hot, 0)
    slot_rank = jnp.sum(one_hot * (running_count - 1), 1)
    slot_index = flat_ids * capacity + slot_rank
    slot_grid = slot_index.reshape(tok_dev, top_count)
    dispatch = jnp.any(
        slot_grid[None, :, :] == jnp.arange(experts * capacity, dtype=jnp.int32)[:, None, None], -1
    ).astype(jnp.bfloat16)
    outbound = jnp.dot(dispatch, normed, preferred_element_type=jnp.float32).astype(jnp.bfloat16)
    boxed = outbound.reshape(devices, exp_dev, capacity, model_width)
    received = lax.all_to_all(boxed, ("group", "ctx"), split_axis=0, concat_axis=0, tiled=True)
    gate_proj = jnp.einsum(
        "send,edf->senf", received, expert_gate, preferred_element_type=jnp.float32
    )
    up_proj = jnp.einsum("send,edf->senf", received, expert_up, preferred_element_type=jnp.float32)
    activated = (jax.nn.silu(gate_proj) * up_proj).astype(jnp.bfloat16)
    returned = lax.all_to_all(
        jnp.einsum(
            "senf,efd->send", activated, expert_down, preferred_element_type=jnp.float32
        ).astype(jnp.bfloat16),
        ("group", "ctx"),
        split_axis=0,
        concat_axis=0,
        tiled=True,
    )
    returned = returned.reshape(experts * capacity, model_width)
    picked = returned[slot_index].reshape(tok_dev, top_count, model_width).astype(jnp.float32)
    mixing = gate_weights / jnp.sum(gate_weights, -1, keepdims=True)
    expert_sum = jnp.sum(picked * mixing[..., None], 1)
    return (residual.astype(jnp.bfloat16), (residual + expert_sum).astype(jnp.bfloat16))


def solution(mesh):
    in_specs = (
        P(("group", "ctx"), None),
        P(("group", "ctx"), None),
        P(("group", "ctx"), None, None),
        P("group", None, "ctx", None),
        P("group"),
        P("ctx", None),
        P(),
        P(("group", "ctx"), None),
        P(("group", "ctx"), None),
        P(("group", "ctx"), None, None),
        P(("group", "ctx"), None, None),
        P(("group", "ctx"), None, None),
    )
    out_specs = (P(("group", "ctx"), None), P(("group", "ctx"), None))
    return jax.shard_map(body, mesh=mesh, in_specs=in_specs, out_specs=out_specs, check_vma=False)
```

profile of v0, /device:TPU:0, one launch (start us, length us, event | category | flops | bytes accessed | tf_op | source)
XLA Modules:
  0.0 217.1 jit_solution(11206246652855133872)
XLA Ops:
  7.2 1.7 fusion.62
  8.9 0.5 copy.96
  9.5 16.5 %all_gather.3 = bf16[64,4096]{1,0:T(8,128)(2,1)S(1)} all-gather(bf16[8,4096]{1,0:T(8,128)(2,1)S(1)} %copy-done.2), channel_id=1, replica_groups=mesh['group'=4,'ctx'=8] {'ctx'}, dimensions={0}, use_global_device_ids=true | all-gather | bytes 589824 | tf_op jit(solution)/shard_map/all_gather | solution.py:35
  26.1 2.6 %multiply_bitcast_fusion = f32[2,4,8,32,512]{4,3,2,1,0:T(8,128)} fusion(bf16[2,512,4,128,1]{1,3,4,2,0:T(8,128)(2,1)S(1)} %bitcast.118, bf16[2,32,4,8,128]{4,3,2,1,0:T(8,128)(2,1)S(1)} %bitcast.114), kind=kOutput, calls=%fused_computation.14 | convolution fusion | flops 269484032 | bytes 5767168 | tf_op jit(solution)/shard_map/rbkgd,rckd->rkgbc/dot_general | solution.py:43
  28.8 0.8 fusion.37
  29.6 0.4 copy.79
  30.1 2.7 %select_reduce_fusion = f32[2,4,8,32]{3,2,1,0:T(8,128)S(1)} fusion(f32[2,4,8,32,8]{4,3,2,1,0:T(8,128)S(1)} %copy.79, f32[2,4,8,32,512]{4,3,2,1,0:T(8,128)} %multiply_bitcast_fusion, pred[2,520]{1,0:T(4,128)(4,1)S(1)} %pad_add_fusion), kind=kLoop, calls=%fused_computation.3 | loop fusion | flops 3192832 | bytes 4269072 | tf_op jit(solution)/shard_map/reduce_max | solution.py:58
  32.8 29.2 %pmax.7 = f32[2,4,8,32]{3,2,1,0:T(8,128)S(1)} all-reduce(f32[2,4,8,32]{3,2,1,0:T(8,128)S(1)} %select_reduce_fusion), channel_id=1, replica_groups=mesh['group'=4,'ctx'=8] {'ctx'}, use_global_device_ids=true, to_apply=%region_1.2 | all-reduce | flops 2048 | bytes 16384 | tf_op jit(solution)/shard_map/pmax | solution.py:59
  62.0 0.5 copy.98
  62.5 0.7 copy.82
  63.2 2.9 %fusion.8 = f32[2,4,8,32,128]{4,3,2,1,0:T(8,128)S(1)} fusion(f32[2,4,8,32,8]{4,3,2,1,0:T(8,128)S(1)} %copy.79, f32[2,4,8,32,512]{4,3,2,1,0:T(8,128)} %multiply_bitcast_fusion, f32[2,4,8,32]{3,2,1,0:T(8,128)S(1)} %pmax.7, pred[2,520]{1,0:T(4,128)(4,1)S(1)} %pad_add_fusion, bf16[2,8,4,128]{3,1,2,0:T(8,128)(2,1)S(1)} %broadcast_in_dim.43, ...), kind=kOutput, calls=%fused_computation.15 | convolution fusion | flops 279019520 | bytes 6382608 | tf_op jit(solution)/shard_map/rkgbl,rlkd->rkgbd/dot_general | solution.py:65
  66.1 1.1 copy.83
  67.3 0.6 dynamic-slice
  68.5 3.0 %fusion.1 = f32[2,4,8,32]{3,2,1,0:T(8,128)S(1)} fusion(f32[2,4,8,32,8]{4,3,2,1,0:T(8,128)S(1)} %copy.79, f32[2,4,8,32,512]{4,3,2,1,0:T(8,128)} %multiply_bitcast_fusion, f32[2,4,8,32]{3,2,1,0:T(8,128)S(1)} %pmax.7, pred[2,520]{1,0:T(4,128)(4,1)S(1)} %pad_add_fusion), kind=kLoop, calls=%fused_computation.7 | loop fusion | flops 4257792 | bytes 4277264 | tf_op jit(solution)/shard_map/reduce_sum | solution.py:61
  71.6 26.1 %all-reduce = f32[2,32,32]{2,1,0:T(8,128)S(1)} all-reduce(f32[2,32,32]{2,1,0:T(8,128)S(1)} %bitcast.122), channel_id=3, replica_groups=mesh['group'=4,'ctx'=8] {'ctx'}, use_global_device_ids=true, to_apply=%region_4.5.clone | all-reduce | flops 2048 | bytes 16384
  97.8 0.5 reduce-scatter.4.cloned.1.call-done
  98.2 1.0 fusion.52
  99.3 4.0 %fusion.47 = f32[64,4096]{1,0:T(8,128)} fusion(bf16[512,4096]{1,0:T(8,128)(2,1)} %param.17, bf16[8,8,4,128]{3,2,1,0:T(4,128)(2,1)S(1)} %bitcast.121), kind=kOutput, calls=%fused_computation.47 | convolution fusion | flops 268435456 | bytes 5308416 | tf_op jit(solution)/shard_map/dot_general | solution.py:79
  104.0 30.4 %reduce-scatter.6.cloned.1.call-done = f32[8,4096]{1,0:T(8,128)} async-done(((f32[64,4096]{1,0:T(8,128)}), f32[8,4096]{1,0:T(8,128)}) %reduce-scatter.6.cloned.1.call-update) | async-done | bytes 131088 | tf_op jit(solution)/shard_map/reduce_scatter | solution.py:78
  134.4 1.1 multiply_reduce_fusion
  135.5 1.4 convolution_convert_fusion.1
  136.9 0.4 reshape.124
  137.3 30.0 %all_to_all.10 = bf16[32,1,4,4096]{3,2,1,0:T(4,128)(2,1)S(1)} all-to-all(bf16[32,1,4,4096]{3,2,1,0:T(4,128)(2,1)S(1)} %bitcast.117), channel_id=1, replica_groups=mesh['group'=4,'ctx'=8] {'group','ctx'}, dimensions={0} | all-to-all | bytes 2097152 | tf_op jit(solution)/shard_map/all_to_all | solution.py:103
  167.3 3.4 %fusion.11 = f32[32,1,4,512]{3,0,2,1:T(8,128)S(1)} fusion(bf16[1,4096,512]{2,1,0:T(8,128)(2,1)} %param.21, bf16[32,1,4,4096]{3,2,1,0:T(4,128)(2,1)S(1)} %all_to_all.10), kind=kOutput, calls=%fused_computation.17 | convolution fusion | flops 536870912 | bytes 5505024 | tf_op jit(solution)/shard_map/send,edf->senf/dot_general | solution.py:104
  170.7 5.4 %fusion = bf16[32,1,4,4096]{3,0,2,1:T(8,128)(2,1)S(1)} fusion(bf16[1,512,4096]{2,1,0:T(8,128)(2,1)} %param.23, bf16[1,4096,512]{2,1,0:T(8,128)(2,1)} %param.22, bf16[32,1,4,4096]{3,2,1,0:T(4,128)(2,1)S(1)} %all_to_all.10, f32[32,1,4,512]{3,0,2,1:T(8,128)S(1)} %fusion.11), kind=kOutput, calls=%fused_computation.6 | convolution fusion | flops 1074659328 | bytes 10747904 | tf_op jit(solution)/shard_map/senf,efd->send/dot_general | solution.py:110
  176.1 1.8 copy.88
  177.9 2.6 %all-to-all-start.1 = ((bf16[32,1,4,4096]{3,2,1,0:T(4,128)(2,1)}), bf16[32,1,4,4096]{3,2,1,0:T(4,128)(2,1)S(1)}, u32[]{:S(2)}, u32[]{:S(2)}) async-start(bf16[32,1,4,4096]{3,2,1,0:T(4,128)(2,1)} %copy.88), calls=%async_computation.3 | async-start | bytes 2097152 | tf_op jit(solution)/shard_map/all_to_all | solution.py:109
  180.8 27.2 %all-to-all-done.1 = bf16[32,1,4,4096]{3,2,1,0:T(4,128)(2,1)S(1)} async-done(((bf16[32,1,4,4096]{3,2,1,0:T(4,128)(2,1)}), bf16[32,1,4,4096]{3,2,1,0:T(4,128)(2,1)S(1)}, u32[]{:S(2)}, u32[]{:S(2)}) %all-to-all-start.1) | async-done | bytes 1048608 | tf_op jit(solution)/shard_map/all_to_all | solution.py:109
  208.0 0.3 reshape.130
  208.3 0.9 gather_fusion
  209.1 0.4 fusion.28
  209.6 0.7 add_convert_fusion
  (48 shorter events, 1.4 us)
Async XLA Ops:
  7.2 2.3 %copy-start.2 = (bf16[8,4096]{1,0:T(8,128)(2,1)S(1)}, bf16[8,4096]{1,0:T(8,128)(2,1)}, u32[]{:S(2)}) copy-start(bf16[8,4096]{1,0:T(8,128)(2,1)} %param.13) | copy-start | bytes 196612
  7.2 18.9 %copy-start.3 = (bf16[8,2,512]{2,1,0:T(2,128)(2,1)S(1)}, bf16[8,2,512]{2,1,0:T(2,128)(2,1)}, u32[]{:S(2)}) copy-start(bf16[8,2,512]{2,1,0:T(2,128)(2,1)} %param.14) | copy-start | bytes 49156
  7.2 91.0 %reduce-scatter.4.cloned.1.call-start = ((), (), s32[]{:S(2)}) async-start(), calls=%async_computation.4 | async-start | bytes 1179648 | tf_op jit(solution)/shard_map/reduce_scatter | solution.py:73
  26.1 3.9 %copy-start.7 = (s32[2]{0:T(128)S(1)}, s32[2]{0:T(128)}, u32[]{:S(2)}) copy-start(s32[2]{0:T(128)} %param.16) | copy-start | bytes 28
  63.2 4.1 %copy-start.8 = (u32[32]{0:T(128)S(1)}, u32[32]{0:T(128)}, u32[]{:S(2)}) copy-start(u32[32]{0:T(128)} %constant.65) | copy-start | bytes 388
  67.2 67.2 %reduce-scatter.6.cloned.1.call-start = ((), (), s32[]{:S(2)}) async-start(), calls=%async_computation.5 | async-start | bytes 1179648 | tf_op jit(solution)/shard_map/reduce_scatter | solution.py:78
  71.6 31.8 %copy-start.6 = (s32[8,8]{1,0:T(8,128)S(1)}, s32[8,8]{1,0:T(8,128)}, u32[]{:S(2)}) copy-start(s32[8,8]{1,0:T(8,128)} %param.19) | copy-start | bytes 772
  71.6 62.8 %copy-start.1 = (bf16[8,4096]{1,0:T(8,128)(2,1)S(1)}, bf16[8,4096]{1,0:T(8,128)(2,1)}, u32[]{:S(2)}) copy-start(bf16[8,4096]{1,0:T(8,128)(2,1)} %param.12) | copy-start | bytes 196612
  71.6 63.9 %copy-start.4 = (f32[4096]{0:T(1024)S(1)}, f32[4096]{0:T(1024)}, u32[]{:S(2)}) copy-start(f32[4096]{0:T(1024)} %param.18) | copy-start | bytes 49156
  176.0 4.6 %copy-start.5 = (f32[8,8]{1,0:T(8,128)S(1)}, f32[8,8]{1,0:T(8,128)}, u32[]{:S(2)}) copy-start(f32[8,8]{1,0:T(8,128)} %param.20) | copy-start | bytes 772
  177.9 30.1 %all-to-all-start.1 = ((bf16[32,1,4,4096]{3,2,1,0:T(4,128)(2,1)}), bf16[32,1,4,4096]{3,2,1,0:T(4,128)(2,1)S(1)}, u32[]{:S(2)}, u32[]{:S(2)}) async-start(bf16[32,1,4,4096]{3,2,1,0:T(4,128)(2,1)} %copy.88), calls=%async_computation.3 | async-start | bytes 2097152 | tf_op jit(solution)/shard_map/all_to_all | solution.py:109
  180.5 29.1 %copy-start = (f32[8,4096]{1,0:T(8,128)S(1)}, f32[8,4096]{1,0:T(8,128)}, u32[]{:S(2)}) copy-start(f32[8,4096]{1,0:T(8,128)} %reduce-scatter.6.cloned.1.call-done) | copy-start | bytes 393220
Sparse Core Ops, SparseCore 0:
  67.3 30.8 reduce-scatter.3
  103.5 30.8 reduce-scatter.5
where the time goes:
time: 218 us; the launch traced here: 217 us
  blocking collectives  102 us (47%)
  waiting for transfers between devices  58.1 us (27%)
  matrix products  20.5 us (9%)
  between operations  15 us (7%)
  other arithmetic  9.73 us (4%)
  local copies, waits for them, and re-layouts  9.28 us (4%)
  starting transfers between devices  2.72 us (1%)
    reduce_scatter x1, waiting for transfers between devices, body(): lax.psum_scatter(jnp.dot(heads_out, out_proj, preferred_element_type=jnp....  30.4 us
    all_to_all x1, blocking collectives, body(): lax.all_to_all(boxed, ('group', 'ctx'), split_axis=0, concat_axis=0, tile...  30 us
    pmax x1, blocking collectives, body(): maximum = lax.pmax(local_peak, 'ctx')  29.2 us
    all_to_all x1, waiting for transfers between devices, body(): lax.all_to_all(jnp.einsum('senf,efd->send', activated, expert_down, prefe...  27.2 us
    unnamed x1, blocking collectives  26.1 us
    all_gather x1, blocking collectives, body(): gathered = lax.all_gather(queries, 'ctx', axis=0, tiled=True)  16.5 us
    dot_general x1, matrix products, body(): jnp.einsum('senf,efd->send', activated, expert_down, preferred_element_ty...  5.35 us
  transfers between devices with their start and end apart: 3, of which 3 were waited for; matrix products, arithmetic and copies ran while one was open for 2% of the time, Pallas kernels for 0%

commit v1 on v0

v1 whole, which is shorter than its diff:
```python
import functools

import jax
import jax.numpy as jnp
from jax import lax
from jax.experimental import pallas as pl
from jax.experimental.pallas import tpu as pltpu
from jax.sharding import Mesh
from jax.sharding import PartitionSpec as P

HEAD_DIM = 128
BLOCK = 32
LANES = 128
FLOOR = -1e30

VMEM = pl.BlockSpec(memory_space=pltpu.VMEM)
SMEM = pl.BlockSpec(memory_space=pltpu.SMEM)
F32 = jnp.float32
BF16 = jnp.bfloat16


def call(kernel, outs, n_in, limit, smem=(), scratch=(), flops=0, moved=0, name=None):
    specs = [SMEM if i in smem else VMEM for i in range(n_in)]
    return pl.pallas_call(
        kernel,
        out_shape=outs,
        in_specs=specs,
        out_specs=jax.tree.map(lambda _: VMEM, outs),
        scratch_shapes=list(scratch),
        compiler_params=pltpu.CompilerParams(vmem_limit_bytes=limit << 20),
        cost_estimate=pl.CostEstimate(flops=flops, bytes_accessed=moved, transcendentals=0),
        name=name,
    )


def shape(dims, dtype):
    return jax.ShapeDtypeStruct(tuple(dims), dtype)


def attend(geo, *refs):
    nz, tok, hd, group_size, chips_per_request = geo
    slots = 2 * nz
    q_refs = refs[:slots]
    cache_ref, block_ref, len_ref, keep_ref, send_ref, kb_ref, vb_ref = refs[slots:]
    z, core = lax.axis_index("z"), lax.axis_index("core")
    cache_dev = cache_ref.shape[2]
    scale = HEAD_DIM ** (-0.5)
    first = (2 * z + core) * cache_dev
    kb_ref[...] = jnp.zeros_like(kb_ref)
    vb_ref[...] = jnp.zeros_like(vb_ref)
    kb_ref[0:tok, :] = block_ref[:, 0, :].astype(F32)
    vb_ref[0:tok, :] = block_ref[:, 1, :].astype(F32)
    span = 2 * chips_per_request * tok
    piece = chips_per_request * tok
    rows = 2 * hd * span
    column = lax.broadcasted_iota(jnp.int32, (rows, cache_dev), 1)
    block_valid = lax.broadcasted_iota(jnp.int32, (rows, LANES), 1) < tok
    lane = lax.broadcasted_iota(jnp.int32, (span, LANES), 1)

    def chip(k, carry):
        there = jnp.bitwise_xor(z, k)
        kv = pl.multiple_of(lax.div(there * (2 * hd), group_size) * HEAD_DIM, HEAD_DIM)
        for rr in range(nz // chips_per_request):
            request = jnp.bitwise_xor(lax.div(z, chips_per_request), rr)
            parts = []
            for half in range(2):
                for h in range(hd):
                    head = (2 * there + jnp.bitwise_xor(core, half)) * hd + h
                    at = pl.multiple_of(head * HEAD_DIM, HEAD_DIM)
                    for dc in range(2):
                        for kk in range(chips_per_request):
                            slot = q_refs[dc * nz + rr * chips_per_request + kk]
                            parts.append(slot[:, pl.ds(at, HEAD_DIM)].astype(F32))
            query = jnp.concatenate(parts, 0).astype(BF16)
            keys = cache_ref[request, 0, :, pl.ds(kv, HEAD_DIM)]
            values = cache_ref[request, 1, :, pl.ds(kv, HEAD_DIM)]
            contract = (((1,), (1,)), ((), ()))
            scores = lax.dot_general(query, keys, contract, preferred_element_type=F32) * scale
            allowed = column < len_ref[request] - first
            scores = jnp.where(allowed, scores, FLOOR)
            peak = jnp.max(scores, -1, keepdims=True)
            if rr == 0:
                block_keys = kb_ref[:, pl.ds(kv, HEAD_DIM)].astype(BF16)
                block_scores = (
                    lax.dot_general(query, block_keys, contract, preferred_element_type=F32) * scale
                )
                block_scores = jnp.where(block_valid, block_scores, FLOOR)
                peak = jnp.maximum(peak, jnp.max(block_scores, -1, keepdims=True))
            peak = peak.astype(BF16).astype(F32)
            probs = jnp.where(allowed, jnp.exp(scores - peak), 0.0)
            total = jnp.sum(probs, -1, keepdims=True)
            summed = jnp.dot(probs.astype(BF16), values, preferred_element_type=F32)
            if rr == 0:
                block_probs = jnp.where(block_valid, jnp.exp(block_scores - peak), 0.0)
                total = total + jnp.sum(block_probs, -1, keepdims=True)
                block_values = vb_ref[:, pl.ds(kv, HEAD_DIM)].astype(BF16)
                summed = summed + jnp.dot(
                    block_probs.astype(BF16), block_values, preferred_element_type=F32
                )
            total_high = total.astype(BF16).astype(F32)
            total_low = total - total_high
            for half, out_ref in ((0, keep_ref), (1, send_ref)):
                stats = jnp.zeros((span, LANES), F32)
                for h in range(hd):
                    at = (half * hd + h) * span
                    chunk = summed[at : at + span].astype(BF16)
                    for dc in range(2):
                        to = dc * nz * tok + rr * piece
                        out_ref[k, to : to + piece, h * HEAD_DIM : (h + 1) * HEAD_DIM] = chunk[
                            dc * piece : (dc + 1) * piece
                        ]
                    stats = jnp.where(lane == h, peak[at : at + span], stats)
                    stats = jnp.where(lane == hd + h, total_high[at : at + span], stats)
                    stats = jnp.where(lane == 2 * hd + h, total_low[at : at + span], stats)
                stats = stats.astype(BF16)
                for dc in range(2):
                    to = dc * nz * tok + rr * piece
                    out_ref[k, to : to + piece, hd * HEAD_DIM :] = stats[
                        dc * piece : (dc + 1) * piece
                    ]
        return carry

    lax.fori_loop(0, nz, chip, 0, unroll=nz <= 4)


def realigned(view, flip, k, nz, tok):
    view = view.astype(F32)
    order = [((dc ^ flip) * nz + (kk ^ k)) * tok for dc in range(2) for kk in range(nz)]
    return jnp.concatenate([view[at : at + tok] for at in order], 0)


def merged(views, hd):
    stats = [v[:, hd * HEAD_DIM :] for v in views]
    numerators, totals, peaks = [], [], []
    for h in range(hd):
        peak = [s[:, h : h + 1] for s in stats]
        total = [s[:, hd + h : hd + h + 1] + s[:, 2 * hd + h : 2 * hd + h + 1] for s in stats]
        top = functools.reduce(jnp.maximum, peak)
        factor = [jnp.exp(p - top) for p in peak]
        cut = slice(h * HEAD_DIM, (h + 1) * HEAD_DIM)
        numerators.append(sum(f * v[:, cut] for f, v in zip(factor, views)))
        totals.append(sum(f * t for f, t in zip(factor, total)))
        peaks.append(top)
    return numerators, totals, peaks


def merge_pair(hd, nz, tok, keep_ref, got_ref, *out_refs):
    rows = keep_ref.shape[1]
    lane = lax.broadcasted_iota(jnp.int32, (rows, LANES), 1)
    for k in range(nz):
        numerators, totals, peaks = merged(
            [keep_ref[k].astype(F32), realigned(got_ref[k], 1, 0, nz, tok)], hd
        )
        stats = jnp.zeros((rows, LANES), F32)
        for h in range(hd):
            high = totals[h].astype(BF16).astype(F32)
            stats = jnp.where(lane == h, peaks[h], stats)
            stats = jnp.where(lane == hd + h, high, stats)
            stats = jnp.where(lane == 2 * hd + h, totals[h] - high, stats)
            out_refs[k][:, h * HEAD_DIM : (h + 1) * HEAD_DIM] = numerators[h].astype(BF16)
        out_refs[k][:, hd * HEAD_DIM :] = stats.astype(BF16)


def project(hd, nz, tok, *refs):
    slots, (w_ref, keep_ref, send_ref) = refs[:nz], refs[nz:]
    numerators, totals, _ = merged([realigned(s[...], 0, k, nz, tok) for k, s in enumerate(slots)], hd)
    heads = jnp.concatenate([n / t for n, t in zip(numerators, totals)], 1)
    high = heads.astype(BF16)
    low = (heads - high.astype(F32)).astype(BF16)
    rows = heads.shape[0]
    half = rows // 2
    heads = jnp.concatenate([high, low], 0)
    width = w_ref.shape[1]
    step = min(width, 1024)
    for at in range(0, width, step):
        out = jnp.dot(heads, w_ref[:, at : at + step], preferred_element_type=F32)
        out = out[:rows] + out[rows:]
        keep_ref[:, at : at + step] = out[:half]
        send_ref[:, at : at + step] = out[half:]


def add_pair(nz, tok, keep_ref, got_ref, own_ref, *out_refs):
    total = keep_ref[...] + got_ref[...].astype(F32)
    own_ref[...] = total[:tok]
    for k in range(1, nz):
        out_refs[k - 1][...] = total[k * tok : (k + 1) * tok].astype(BF16)


def normalize(nz, experts, *refs):
    hidden_ref, own_ref = refs[:2]
    got = refs[2 : nz + 1]
    gain_ref, ids_ref, gates_ref, attended_ref, residual_ref, out_ref = refs[nz + 1 :]
    attention = own_ref[...]
    for ref in got:
        attention = attention + ref[...].astype(F32)
    residual = hidden_ref[...].astype(F32) + attention
    residual_ref[...] = residual
    attended_ref[...] = residual.astype(BF16)
    mean_square = jnp.mean(residual * residual, -1, keepdims=True)
    normed = residual * lax.rsqrt(mean_square + 1e-06) * gain_ref[...]
    width = residual.shape[1]
    out_ref[:, :width] = normed.astype(BF16)
    gates = gates_ref[...]
    mixing = gates / jnp.sum(gates, -1, keepdims=True)
    high = mixing.astype(BF16).astype(F32)
    low = mixing - high
    ids = ids_ref[...]
    extra = out_ref.shape[1] - width
    lane = lax.broadcasted_iota(jnp.int32, (residual.shape[0], extra), 1)
    mix = jnp.zeros((residual.shape[0], extra), F32)
    for k in range(ids.shape[1]):
        expert = ids[:, k : k + 1]
        mix = jnp.where(lane == expert, high[:, k : k + 1], mix)
        mix = jnp.where(lane == expert + experts, low[:, k : k + 1], mix)
    out_ref[:, width:] = mix.astype(BF16)


def expert(n_sets, experts, *refs):
    sets = refs[: 2 * n_sets]
    gate_ref, up_ref, down_ref = refs[2 * n_sets : 2 * n_sets + 3]
    keeps = refs[2 * n_sets + 3 : 3 * n_sets + 3]
    sends = refs[3 * n_sets + 3 : 4 * n_sets + 3]
    mine = (lax.axis_index("group") * lax.axis_size("z") + lax.axis_index("z")) * 2 + lax.axis_index("core")
    rows = sets[0].shape[0]
    width = gate_ref.shape[1]
    per = max(1, 256 // rows)
    for start in range(0, 2 * n_sets, per):
        held = [s[...] for s in sets[start : start + per]]
        x = jnp.concatenate([h[:, :width] for h in held], 0)
        mix = jnp.concatenate([h[:, width:] for h in held], 0).astype(F32)
        lane = lax.broadcasted_iota(jnp.int32, mix.shape, 1)
        chosen = (lane == mine) | (lane == mine + experts)
        mix = jnp.sum(jnp.where(chosen, mix, 0.0), -1, keepdims=True)
        gate = jnp.dot(x, gate_ref[0], preferred_element_type=F32)
        up = jnp.dot(x, up_ref[0], preferred_element_type=F32)
        activated = (gate / (1.0 + jnp.exp(-gate)) * up).astype(BF16)
        step = min(width, 1024)
        for at in range(0, width, step):
            out = jnp.dot(activated, down_ref[0, :, at : at + step], preferred_element_type=F32)
            out = out.astype(BF16).astype(F32) * mix
            out = out.astype(BF16)
            for i in range(len(held)):
                s = start + i
                ref = keeps[s] if s < n_sets else sends[s - n_sets]
                ref[:, at : at + step] = out[i * rows : (i + 1) * rows]


def add_all(n, split, *refs):
    total = refs[0][...].astype(F32)
    for ref in refs[1:n]:
        total = total + ref[...].astype(F32)
    outs = refs[n:]
    if split is None:
        outs[0][...] = total.astype(outs[0].dtype)
        return
    for k, out in enumerate(outs):
        out[...] = total[k * split : (k + 1) * split].astype(out.dtype)


def swap(x, axis, k, n):
    return lax.ppermute(x, axis, [(i, i ^ k) for i in range(n)])


def body(hidden_in, queries, block_kv, cache, lengths, out_proj, norm_gain, expert_ids, gate_weights, expert_gate, expert_up, expert_down):
    nz, ng = lax.axis_size("z"), lax.axis_size("group")
    tok, width = hidden_in.shape
    requests, _, cache_dev, kv_width = cache.shape
    num_heads = queries.shape[1] // HEAD_DIM
    group_size = num_heads * HEAD_DIM // kv_width
    hd = num_heads // (2 * nz)
    cpr = BLOCK // (2 * tok)
    experts = expert_gate.shape[0] * ng * nz * 2
    tokens = 2 * nz * tok
    block_kv = block_kv

    mine = [queries] + [swap(queries, "z", k, nz) for k in range(1, nz)]
    other = [swap(q, "core", 1, 2) for q in mine]
    slot = hd * HEAD_DIM + LANES
    part = shape((nz, tokens, slot), BF16)
    keep, send = call(
        functools.partial(attend, (nz, tok, hd, group_size, cpr)),
        (part, part),
        2 * nz + 3,
        24,
        smem=(2 * nz + 2,),
        scratch=[pltpu.VMEM((LANES, kv_width), F32)] * 2,
        flops=4 * tokens * num_heads * HEAD_DIM * cache_dev,
        moved=cache.size * 2,
        name="attend",
    )(*mine, *other, cache, block_kv, lengths)
    got = swap(send, "core", 1, 2)
    pairs = call(
        functools.partial(merge_pair, hd, nz, tok),
        [shape((tokens, slot), BF16)] * nz,
        2,
        12,
        name="merge_pair",
    )(keep, got)
    slots = [pairs[0]] + [swap(pairs[k], "z", k, nz) for k in range(1, nz)]
    keep, send = call(
        functools.partial(project, hd, nz, tok),
        (shape((tokens // 2, width), F32), shape((tokens // 2, width), F32)),
        nz + 1,
        16,
        flops=2 * tokens * out_proj.size,
        moved=out_proj.size * 2,
        name="project",
    )(*slots, out_proj)
    got = swap(send, "core", 1, 2)
    own, *away = call(
        functools.partial(add_pair, nz, tok),
        [shape((tok, width), F32)] + [shape((tok, width), BF16)] * (nz - 1),
        2,
        12,
        name="add_pair",
    )(keep, got)
    got = [swap(away[k - 1], "z", k, nz) for k in range(1, nz)]
    extra = -(-2 * experts // LANES) * LANES
    attended, residual, normed = call(
        functools.partial(normalize, nz, experts),
        (shape((tok, width), BF16), shape((tok, width), F32), shape((tok, width + extra), BF16)),
        nz + 4,
        8,
        name="normalize",
    )(hidden_in, own, *got, norm_gain.reshape(1, width), expert_ids, gate_weights)
    column = [normed] + [swap(normed, "z", k, nz) for k in range(1, nz)]
    column = jnp.concatenate(column, 0)
    near = [column] + [swap(column, "group", g, ng) for g in range(1, ng)]
    far = [swap(c, "core", 1, 2) for c in near]
    rows = nz * tok
    outs = call(
        functools.partial(expert, ng, experts),
        [shape((rows, width), BF16)] * (2 * ng),
        2 * ng + 3,
        40,
        flops=6 * 2 * ng * rows * expert_gate.size,
        moved=expert_gate.size * 6,
        name="expert",
    )(*near, *far, expert_gate, expert_up, expert_down)
    keeps, sends = outs[:ng], outs[ng:]
    gots = [swap(s, "core", 1, 2) for s in sends]
    sums = [
        call(
            functools.partial(add_all, 2, None),
            [shape((rows, width), F32 if g == 0 else BF16)],
            2,
            8,
            name="add_core",
        )(keeps[g], gots[g])[0]
        for g in range(ng)
    ]
    back = [sums[0]] + [swap(sums[g], "group", g, ng) for g in range(1, ng)]
    own, *away = call(
        functools.partial(add_all, ng, tok),
        [shape((tok, width), F32)] + [shape((tok, width), BF16)] * (nz - 1),
        ng,
        12,
        name="add_group",
    )(*back)
    got = [swap(away[k - 1], "z", k, nz) for k in range(1, nz)]
    layer_out = call(
        functools.partial(add_all, nz + 1, None),
        [shape((tok, width), BF16)],
        nz + 1,
        8,
        name="finish",
    )(residual, own, *got)[0]
    return attended, layer_out


def solution(mesh):
    groups, ctx = mesh.devices.shape
    split = Mesh(mesh.devices.reshape(groups, ctx // 2, 2), ("group", "z", "core"))
    every, across = ("group", "z", "core"), ("z", "core")
    in_specs = (
        P(every, None),
        P(every, None),
        P(every, None, None),
        P("group", None, across, None),
        P("group"),
        P(across, None),
        P(),
        P(every, None),
        P(every, None),
        P(every, None, None),
        P(every, None, None),
        P(every, None, None),
    )
    out_specs = (P(every, None), P(every, None))
    return jax.shard_map(body, mesh=split, in_specs=in_specs, out_specs=out_specs, check_vma=False)
```

time: 218 us -> 108 us (0.50)
  blocking collectives: 102 us -> 0 us
  starting transfers between devices: 2.72 us -> 33.3 us
  matrix products: 20.5 us -> 0 us
  between operations: 15 us -> 0.78 us
  Pallas kernels: 0 us -> 13.5 us
  other arithmetic: 9.73 us -> 0 us
  waiting for transfers between devices: 58.1 us -> 54 us
  local copies, waits for them, and re-layouts: 9.28 us -> 6.06 us
    ppermute x0 -> x35, waiting for transfers between devices: none -> 54 us  [swap(): return lax.ppermute(x, axis, [(i, i ^ k) for i in range(n)])]
    ppermute x0 -> x35, starting transfers between devices: none -> 33.3 us  [swap(): return lax.ppermute(x, axis, [(i, i ^ k) for i in range(n)])]
    reduce_scatter x2 -> x0, waiting for transfers between devices: 30.9 us -> none  [the longest x1 30.4 us: body(): lax.psum_scatter(jnp.dot(heads_out, out_proj, preferred_element_type=jnp....]
    all_to_all x1 -> x0, blocking collectives: 30 us -> none  [body(): lax.all_to_all(boxed, ('group', 'ctx'), split_axis=0, concat_axis=0, tile...]
    pmax x1 -> x0, blocking collectives: 29.2 us -> none  [body(): maximum = lax.pmax(local_peak, 'ctx')]
    all_to_all x1 -> x0, waiting for transfers between devices: 27.2 us -> none  [body(): lax.all_to_all(jnp.einsum('senf,efd->send', activated, expert_down, prefe...]
    unnamed x1 -> x0, blocking collectives: 26.1 us -> none
    dot_general x7 -> x0, matrix products: 20.5 us -> none  [the longest x1 5.35 us: body(): jnp.einsum('senf,efd->send', activated, expert_down, preferred_element_ty...]
  transfers between devices with their start and end apart: 3 -> 35, of which waited for: 3 -> 21; matrix products, arithmetic and copies ran while one was open for 2% -> 0% of each run, Pallas kernels for 0% -> 0%
where the time goes in v1:
time: 108 us
  waiting for transfers between devices  54 us (50%)
  starting transfers between devices  33.3 us (31%)
  Pallas kernels  13.5 us (12%)
  local copies, waits for them, and re-layouts  6.06 us (6%)
    ppermute x35, waiting for transfers between devices, swap(): return lax.ppermute(x, axis, [(i, i ^ k) for i in range(n)])  54 us
    ppermute x35, starting transfers between devices, swap(): return lax.ppermute(x, axis, [(i, i ^ k) for i in range(n)])  33.3 us
    unnamed x25, local copies, waits for them, and re-layouts  6.04 us
    pallas_call x1, Pallas kernels, body(): call(functools.partial(expert, ng, experts), [shape((rows, width), BF16)]...  5.69 us
    pallas_call x1, Pallas kernels, body(): call(functools.partial(attend, (nz, tok, hd, group_size, cpr)), (part, pa...  3.8 us
  transfers between devices with their start and end apart: 35, of which 21 were waited for; matrix products, arithmetic and copies ran while one was open for 0% of the time, Pallas kernels for 0%

profile of v1, /device:TPU:0, one launch (start us, length us, event | category | flops | bytes accessed | tf_op | source)
XLA Modules:
  0.0 107.6 jit_solution(4300284609811070969)
XLA Ops:
  0.6 5.1 %collective-permute-start.2 = (bf16[8,4096]{1,0:T(8,128)(2,1)}, bf16[8,4096]{1,0:T(8,128)(2,1)S(1)}, u32[]{:S(2)}, u32[]{:S(2)}) collective-permute-start(bf16[8,4096]{1,0:T(8,128)(2,1)} %refs_0_.2), channel_id=1, source_target_pairs={{0,6},{2,4},{4,2},{6,0},{1,7},{3,5},{5,3},{7,1},{8,14},{10,12},{12... | collective-permute-start | bytes 196616 | tf_op jit(solution)/shard_map/ppermute | solution.py:261
  6.4 2.2 %collective-permute-done.2.refs_3_ = bf16[8,4096]{1,0:T(8,128)(2,1)S(1)} collective-permute-done((bf16[8,4096]{1,0:T(8,128)(2,1)}, bf16[8,4096]{1,0:T(8,128)(2,1)S(1)}, u32[]{:S(2)}, u32[]{:S(2)}) %collective-permute-start.2) | collective-permute-done | bytes 65568 | tf_op jit(solution)/shard_map/ppermute | solution.py:261
  8.6 3.0 %collective-permute-done.1.refs_2_ = bf16[8,4096]{1,0:T(8,128)(2,1)S(1)} collective-permute-done((bf16[8,4096]{1,0:T(8,128)(2,1)}, bf16[8,4096]{1,0:T(8,128)(2,1)S(1)}, u32[]{:S(2)}, u32[]{:S(2)}) %collective-permute-start.1) | collective-permute-done | bytes 65568 | tf_op jit(solution)/shard_map/ppermute | solution.py:261
  13.0 1.6 %copy-done.3 = bf16[2,2,512,512]{3,2,1,0:T(8,128)(2,1)S(1)} copy-done((bf16[2,2,512,512]{3,2,1,0:T(8,128)(2,1)S(1)}, bf16[2,2,512,512]{3,2,1,0:T(8,128)(2,1)}, u32[]{:S(2)}) %copy-start.3) | copy-done | bytes 2097176
  16.8 3.8 %attend.1 = (bf16[4,64,640]{2,1,0:T(8,128)(2,1)S(1)}, bf16[4,64,640]{2,1,0:T(8,128)(2,1)S(1)}) custom-call(bf16[8,4096]{1,0:T(8,128)(2,1)S(1)} %copy-done.4, bf16[8,4096]{1,0:T(8,128)(2,1)S(1)} %collective-permute-done.refs_1_, bf16[8,4096]{1,0:T(8,128)(2,1)S(1)} %collective-permute-done.1.refs_2_, bf16[8,4096]{1,0:T(8,128)(2,1)S(1)} %collective-permute-done.2.refs_3_, ...), custom_call_target="tpu_custom_call" | custom-call | flops 536870912 | bytes 2097152 | tf_op jit(solution)/shard_map/attend/pallas_call | solution.py:280
  21.1 1.3 %collective-permute-done.7.got_ref = bf16[4,64,640]{2,1,0:T(8,128)(2,1)S(1)} collective-permute-done((bf16[4,64,640]{2,1,0:T(8,128)(2,1)S(1)}, bf16[4,64,640]{2,1,0:T(8,128)(2,1)S(1)}, u32[]{:S(2)}, u32[]{:S(2)}) %collective-permute-start.7) | collective-permute-done | bytes 327712 | tf_op jit(solution)/shard_map/ppermute | solution.py:261
  22.3 1.2 %merge_pair.1 = (bf16[64,640]{1,0:T(8,128)(2,1)S(1)}, bf16[64,640]{1,0:T(8,128)(2,1)S(1)}, bf16[64,640]{1,0:T(8,128)(2,1)S(1)}, bf16[64,640]{1,0:T(8,128)(2,1)S(1)}) custom-call(bf16[4,64,640]{2,1,0:T(8,128)(2,1)S(1)} %get-tuple-element.29.keep_ref, bf16[4,64,640]{2,1,0:T(8,128)(2,1)S(1)} %collective-permute-done.7.got_ref), custom_call_target="tpu_custom_call" | custom-call | tf_op jit(solution)/shard_map/merge_pair/pallas_call | solution.py:292
  24.5 2.3 %collective-permute-start.9 = (bf16[64,640]{1,0:T(8,128)(2,1)S(1)}, bf16[64,640]{1,0:T(8,128)(2,1)S(1)}, u32[]{:S(2)}, u32[]{:S(2)}) collective-permute-start(bf16[64,640]{1,0:T(8,128)(2,1)S(1)} %get-tuple-element.33), channel_id=1, source_target_pairs={{0,4},{2,6},{4,0},{6,2},{1,5},{3,7},{5,1},{7,3},{8,12},{10,14},{12... | collective-permute-start | bytes 245768 | tf_op jit(solution)/shard_map/ppermute | solution.py:261
  26.8 1.1 %collective-permute-start.10 = (bf16[64,640]{1,0:T(8,128)(2,1)S(1)}, bf16[64,640]{1,0:T(8,128)(2,1)S(1)}, u32[]{:S(2)}, u32[]{:S(2)}) collective-permute-start(bf16[64,640]{1,0:T(8,128)(2,1)S(1)} %get-tuple-element.34), channel_id=1, source_target_pairs={{0,6},{2,4},{4,2},{6,0},{1,7},{3,5},{5,3},{7,1},{8,14},{10,12},{12... | collective-permute-start | bytes 245768 | tf_op jit(solution)/shard_map/ppermute | solution.py:261
  27.9 1.3 %collective-permute-done.8.refs_1_ = bf16[64,640]{1,0:T(8,128)(2,1)S(1)} collective-permute-done((bf16[64,640]{1,0:T(8,128)(2,1)S(1)}, bf16[64,640]{1,0:T(8,128)(2,1)S(1)}, u32[]{:S(2)}, u32[]{:S(2)}) %collective-permute-start.8) | collective-permute-done | bytes 81952 | tf_op jit(solution)/shard_map/ppermute | solution.py:261
  29.2 4.8 %collective-permute-done.9.refs_2_ = bf16[64,640]{1,0:T(8,128)(2,1)S(1)} collective-permute-done((bf16[64,640]{1,0:T(8,128)(2,1)S(1)}, bf16[64,640]{1,0:T(8,128)(2,1)S(1)}, u32[]{:S(2)}, u32[]{:S(2)}) %collective-permute-start.9) | collective-permute-done | bytes 81952 | tf_op jit(solution)/shard_map/ppermute | solution.py:261
  34.1 2.2 %copy-done.2 = bf16[512,4096]{1,0:T(8,128)(2,1)S(1)} copy-done((bf16[512,4096]{1,0:T(8,128)(2,1)S(1)}, bf16[512,4096]{1,0:T(8,128)(2,1)}, u32[]{:S(2)}) %copy-start.2) | copy-done | bytes 4194328
  37.4 1.9 %collective-permute-done.11.got_ref = f32[32,4096]{1,0:T(8,128)S(1)} collective-permute-done((f32[32,4096]{1,0:T(8,128)S(1)}, f32[32,4096]{1,0:T(8,128)S(1)}, u32[]{:S(2)}, u32[]{:S(2)}) %collective-permute-start.11) | collective-permute-done | bytes 524320 | tf_op jit(solution)/shard_map/ppermute | solution.py:261
  39.3 1.6 %collective-permute-start.12 = (bf16[8,4096]{1,0:T(8,128)(2,1)S(1)}, bf16[8,4096]{1,0:T(8,128)(2,1)S(1)}, u32[]{:S(2)}, u32[]{:S(2)}) collective-permute-start(bf16[8,4096]{1,0:T(8,128)(2,1)S(1)} %get-tuple-element.38), channel_id=1, source_target_pairs={{0,2},{2,0},{4,6},{6,4},{1,3},{3,1},{5,7},{7,5},{8,10},{10,8},{12,... | collective-permute-start | bytes 196616 | tf_op jit(solution)/shard_map/ppermute | solution.py:261
  40.9 1.2 %collective-permute-start.13 = (bf16[8,4096]{1,0:T(8,128)(2,1)S(1)}, bf16[8,4096]{1,0:T(8,128)(2,1)S(1)}, u32[]{:S(2)}, u32[]{:S(2)}) collective-permute-start(bf16[8,4096]{1,0:T(8,128)(2,1)S(1)} %get-tuple-element.39), channel_id=1, source_target_pairs={{0,4},{2,6},{4,0},{6,2},{1,5},{3,7},{5,1},{7,3},{8,12},{10,14},{12... | collective-permute-start | bytes 196616 | tf_op jit(solution)/shard_map/ppermute | solution.py:261
  42.1 1.7 %collective-permute-start.14 = (bf16[8,4096]{1,0:T(8,128)(2,1)S(1)}, bf16[8,4096]{1,0:T(8,128)(2,1)S(1)}, u32[]{:S(2)}, u32[]{:S(2)}) collective-permute-start(bf16[8,4096]{1,0:T(8,128)(2,1)S(1)} %get-tuple-element.40), channel_id=1, source_target_pairs={{0,6},{2,4},{4,2},{6,0},{1,7},{3,5},{5,3},{7,1},{8,14},{10,12},{12... | collective-permute-start | bytes 196616 | tf_op jit(solution)/shard_map/ppermute | solution.py:261
  43.8 5.3 %collective-permute-done.13.refs_3_ = bf16[8,4096]{1,0:T(8,128)(2,1)S(1)} collective-permute-done((bf16[8,4096]{1,0:T(8,128)(2,1)S(1)}, bf16[8,4096]{1,0:T(8,128)(2,1)S(1)}, u32[]{:S(2)}, u32[]{:S(2)}) %collective-permute-start.13) | collective-permute-done | bytes 65568 | tf_op jit(solution)/shard_map/ppermute | solution.py:261
  49.9 2.1 %collective-permute-start.17 = (bf16[8,4224]{1,0:T(8,128)(2,1)S(1)}, bf16[8,4224]{1,0:T(8,128)(2,1)S(1)}, u32[]{:S(2)}, u32[]{:S(2)}) collective-permute-start(bf16[8,4224]{1,0:T(8,128)(2,1)S(1)} %get-tuple-element.43), channel_id=1, source_target_pairs={{0,6},{2,4},{4,2},{6,0},{1,7},{3,5},{5,3},{7,1},{8,14},{10,12},{12... | collective-permute-start | bytes 202760 | tf_op jit(solution)/shard_map/ppermute | solution.py:261
  52.6 1.6 %collective-permute-start.15 = (bf16[8,4224]{1,0:T(8,128)(2,1)S(1)}, bf16[8,4224]{1,0:T(8,128)(2,1)S(1)}, u32[]{:S(2)}, u32[]{:S(2)}) collective-permute-start(bf16[8,4224]{1,0:T(8,128)(2,1)S(1)} %get-tuple-element.43), channel_id=1, source_target_pairs={{0,2},{2,0},{4,6},{6,4},{1,3},{3,1},{5,7},{7,5},{8,10},{10,8},{12,... | collective-permute-start | bytes 202760 | tf_op jit(solution)/shard_map/ppermute | solution.py:261
  54.3 3.1 %collective-permute-done.15 = bf16[8,4224]{1,0:T(8,128)(2,1)S(1)} collective-permute-done((bf16[8,4224]{1,0:T(8,128)(2,1)S(1)}, bf16[8,4224]{1,0:T(8,128)(2,1)S(1)}, u32[]{:S(2)}, u32[]{:S(2)}) %collective-permute-start.15) | collective-permute-done | bytes 67616 | tf_op jit(solution)/shard_map/ppermute | solution.py:261
  57.4 1.1 %collective-permute-done.16 = bf16[8,4224]{1,0:T(8,128)(2,1)S(1)} collective-permute-done((bf16[8,4224]{1,0:T(8,128)(2,1)S(1)}, bf16[8,4224]{1,0:T(8,128)(2,1)S(1)}, u32[]{:S(2)}, u32[]{:S(2)}) %collective-permute-start.16) | collective-permute-done | bytes 67616 | tf_op jit(solution)/shard_map/ppermute | solution.py:261
  58.5 2.5 %collective-permute-start.20 = (bf16[32,4224]{1,0:T(8,128)(2,1)S(1)}, bf16[32,4224]{1,0:T(8,128)(2,1)S(1)}, u32[]{:S(2)}, u32[]{:S(2)}) collective-permute-start(bf16[32,4224]{1,0:T(8,128)(2,1)S(1)} %constant_dynamic-update-slice_fusion.refs_0_), channel_id=1, source_target_pairs={{0,24},{8,16},{16,8},{24,0},{1,25},{9,17},{17,9},{25,1},{2,26},{10... | collective-permute-start | bytes 811016 | tf_op jit(solution)/shard_map/ppermute | solution.py:261
  62.1 6.8 %collective-permute-done.20.refs_3_ = bf16[32,4224]{1,0:T(8,128)(2,1)S(1)} collective-permute-done((bf16[32,4224]{1,0:T(8,128)(2,1)S(1)}, bf16[32,4224]{1,0:T(8,128)(2,1)S(1)}, u32[]{:S(2)}, u32[]{:S(2)}) %collective-permute-start.20) | collective-permute-done | bytes 270368 | tf_op jit(solution)/shard_map/ppermute | solution.py:261
  68.9 3.8 %collective-permute-done.19.refs_2_ = bf16[32,4224]{1,0:T(8,128)(2,1)S(1)} collective-permute-done((bf16[32,4224]{1,0:T(8,128)(2,1)S(1)}, bf16[32,4224]{1,0:T(8,128)(2,1)S(1)}, u32[]{:S(2)}, u32[]{:S(2)}) %collective-permute-start.19) | collective-permute-done | bytes 270368 | tf_op jit(solution)/shard_map/ppermute | solution.py:261
  74.7 5.7 %expert.1 = (bf16[32,4096]{1,0:T(8,128)(2,1)S(1)}, bf16[32,4096]{1,0:T(8,128)(2,1)S(1)}, bf16[32,4096]{1,0:T(8,128)(2,1)S(1)}, bf16[32,4096]{1,0:T(8,128)(2,1)S(...) custom-call(bf16[32,4224]{1,0:T(8,128)(2,1)S(1)} %constant_dynamic-u, ...), custom_call_target="tpu_custom_call" | custom-call | flops 3221225472 | bytes 12582912 | tf_op jit(solution)/shard_map/expert/pallas_call | solution.py:331
  82.0 1.6 %collective-permute-start.27 = (bf16[32,4096]{1,0:T(8,128)(2,1)S(1)}, bf16[32,4096]{1,0:T(8,128)(2,1)S(1)}, u32[]{:S(2)}, u32[]{:S(2)}) collective-permute-start(bf16[32,4096]{1,0:T(8,128)(2,1)S(1)} %add_core.5), channel_id=1, source_target_pairs={{0,8},{8,0},{16,24},{24,16},{1,9},{9,1},{17,25},{25,17},{2,10},{10... | collective-permute-start | bytes 786440 | tf_op jit(solution)/shard_map/ppermute | solution.py:261
  84.6 1.2 %collective-permute-start.31 = (bf16[32,4096]{1,0:T(8,128)(2,1)S(1)}, bf16[32,4096]{1,0:T(8,128)(2,1)S(1)}, u32[]{:S(2)}, u32[]{:S(2)}) collective-permute-start(bf16[32,4096]{1,0:T(8,128)(2,1)S(1)} %add_core.7), channel_id=1, source_target_pairs={{0,24},{8,16},{16,8},{24,0},{1,25},{9,17},{17,9},{25,1},{2,26},{10... | collective-permute-start | bytes 786440 | tf_op jit(solution)/shard_map/ppermute | solution.py:261
  85.9 5.4 %collective-permute-done.27.refs_1_ = bf16[32,4096]{1,0:T(8,128)(2,1)S(1)} collective-permute-done((bf16[32,4096]{1,0:T(8,128)(2,1)S(1)}, bf16[32,4096]{1,0:T(8,128)(2,1)S(1)}, u32[]{:S(2)}, u32[]{:S(2)}) %collective-permute-start.27) | collective-permute-done | bytes 262176 | tf_op jit(solution)/shard_map/ppermute | solution.py:261
  91.3 6.1 %collective-permute-done.29.refs_2_ = bf16[32,4096]{1,0:T(8,128)(2,1)S(1)} collective-permute-done((bf16[32,4096]{1,0:T(8,128)(2,1)S(1)}, bf16[32,4096]{1,0:T(8,128)(2,1)S(1)}, u32[]{:S(2)}, u32[]{:S(2)}) %collective-permute-start.29) | collective-permute-done | bytes 262176 | tf_op jit(solution)/shard_map/ppermute | solution.py:261
  97.6 3.3 %collective-permute-start.33 = (bf16[8,4096]{1,0:T(8,128)(2,1)S(1)}, bf16[8,4096]{1,0:T(8,128)(2,1)S(1)}, u32[]{:S(2)}, u32[]{:S(2)}) collective-permute-start(bf16[8,4096]{1,0:T(8,128)(2,1)S(1)} %get-tuple-element.54), channel_id=1, source_target_pairs={{0,4},{2,6},{4,0},{6,2},{1,5},{3,7},{5,1},{7,3},{8,12},{10,14},{12... | collective-permute-start | bytes 196616 | tf_op jit(solution)/shard_map/ppermute | solution.py:261
  102.0 1.3 %collective-permute-done.33.refs_3_ = bf16[8,4096]{1,0:T(8,128)(2,1)S(1)} collective-permute-done((bf16[8,4096]{1,0:T(8,128)(2,1)S(1)}, bf16[8,4096]{1,0:T(8,128)(2,1)S(1)}, u32[]{:S(2)}, u32[]{:S(2)}) %collective-permute-start.33) | collective-permute-done | bytes 65568 | tf_op jit(solution)/shard_map/ppermute | solution.py:261
  103.3 3.6 %collective-permute-done.34.refs_4_ = bf16[8,4096]{1,0:T(8,128)(2,1)S(1)} collective-permute-done((bf16[8,4096]{1,0:T(8,128)(2,1)S(1)}, bf16[8,4096]{1,0:T(8,128)(2,1)S(1)}, u32[]{:S(2)}, u32[]{:S(2)}) %collective-permute-start.34) | collective-permute-done | bytes 65568 | tf_op jit(solution)/shard_map/ppermute | solution.py:261
  (76 shorter events, 16.0 us)
Async XLA Ops:
  0.6 7.9 %collective-permute-start.2 = (bf16[8,4096]{1,0:T(8,128)(2,1)}, bf16[8,4096]{1,0:T(8,128)(2,1)S(1)}, u32[]{:S(2)}, u32[]{:S(2)}) collective-permute-start(bf16[8,4096]{1,0:T(8,128)(2,1)} %refs_0_.2), channel_id=1, source_target_pairs={{0,6},{2,4},{4,2},{6,0},{1,7},{3,5},{5,3},{7,1},{8,14},{10,12},{12... | collective-permute-start | bytes 196616 | tf_op jit(solution)/shard_map/ppermute | solution.py:261
  5.8 5.8 %collective-permute-start.1 = (bf16[8,4096]{1,0:T(8,128)(2,1)}, bf16[8,4096]{1,0:T(8,128)(2,1)S(1)}, u32[]{:S(2)}, u32[]{:S(2)}) collective-permute-start(bf16[8,4096]{1,0:T(8,128)(2,1)} %refs_0_.2), channel_id=1, source_target_pairs={{0,4},{2,6},{4,0},{6,2},{1,5},{3,7},{5,1},{7,3},{8,12},{10,14},{12... | collective-permute-start | bytes 196616 | tf_op jit(solution)/shard_map/ppermute | solution.py:261
  5.8 5.8 %collective-permute-start = (bf16[8,4096]{1,0:T(8,128)(2,1)}, bf16[8,4096]{1,0:T(8,128)(2,1)S(1)}, u32[]{:S(2)}, u32[]{:S(2)}) collective-permute-start(bf16[8,4096]{1,0:T(8,128)(2,1)} %refs_0_.2), channel_id=1, source_target_pairs={{0,2},{2,0},{4,6},{6,4},{1,3},{3,1},{5,7},{7,5},{8,10},{10,8},{12,... | collective-permute-start | bytes 196616 | tf_op jit(solution)/shard_map/ppermute | solution.py:261
  6.4 5.7 %collective-permute-start.3 = (bf16[8,4096]{1,0:T(8,128)(2,1)}, bf16[8,4096]{1,0:T(8,128)(2,1)S(1)}, u32[]{:S(2)}, u32[]{:S(2)}) collective-permute-start(bf16[8,4096]{1,0:T(8,128)(2,1)} %refs_0_.2), channel_id=1, source_target_pairs={{0,1},{1,0},{2,3},{3,2},{4,5},{5,4},{6,7},{7,6},{8,9},{9,8},{10,11... | collective-permute-start | bytes 196616 | tf_op jit(solution)/shard_map/ppermute | solution.py:261
  8.6 3.5 %collective-permute-start.6 = (bf16[8,4096]{1,0:T(8,128)(2,1)S(1)}, bf16[8,4096]{1,0:T(8,128)(2,1)S(1)}, u32[]{:S(2)}, u32[]{:S(2)}) collective-permute-start(bf16[8,4096]{1,0:T(8,128)(2,1)S(1)} %collective-permute-done.2.refs_3_), channel_id=1, source_target_pairs={{0,1},{1,0},{2,3},{3,2},{4,5},{5,4},{6,7},{7,6},{8,9},{9,8},{10,11... | collective-permute-start | bytes 196616 | tf_op jit(solution)/shard_map/ppermute | solution.py:261
  20.6 1.7 %collective-permute-start.7 = (bf16[4,64,640]{2,1,0:T(8,128)(2,1)S(1)}, bf16[4,64,640]{2,1,0:T(8,128)(2,1)S(1)}, u32[]{:S(2)}, u32[]{:S(2)}) collective-permute-start(bf16[4,64,640]{2,1,0:T(8,128)(2,1)S(1)} %get-tuple-element.30), channel_id=1, source_target_pairs={{0,1},{1,0},{2,3},{3,2},{4,5},{5,4},{6,7},{7,6},{8,9},{9,8},{10,11... | collective-permute-start | bytes 983048 | tf_op jit(solution)/shard_map/ppermute | solution.py:261
  23.5 5.7 %collective-permute-start.8 = (bf16[64,640]{1,0:T(8,128)(2,1)S(1)}, bf16[64,640]{1,0:T(8,128)(2,1)S(1)}, u32[]{:S(2)}, u32[]{:S(2)}) collective-permute-start(bf16[64,640]{1,0:T(8,128)(2,1)S(1)} %get-tuple-element.32), channel_id=1, source_target_pairs={{0,2},{2,0},{4,6},{6,4},{1,3},{3,1},{5,7},{7,5},{8,10},{10,8},{12,... | collective-permute-start | bytes 245768 | tf_op jit(solution)/shard_map/ppermute | solution.py:261
  24.5 9.6 %collective-permute-start.9 = (bf16[64,640]{1,0:T(8,128)(2,1)S(1)}, bf16[64,640]{1,0:T(8,128)(2,1)S(1)}, u32[]{:S(2)}, u32[]{:S(2)}) collective-permute-start(bf16[64,640]{1,0:T(8,128)(2,1)S(1)} %get-tuple-element.33), channel_id=1, source_target_pairs={{0,4},{2,6},{4,0},{6,2},{1,5},{3,7},{5,1},{7,3},{8,12},{10,14},{12... | collective-permute-start | bytes 245768 | tf_op jit(solution)/shard_map/ppermute | solution.py:261
  26.8 7.2 %collective-permute-start.10 = (bf16[64,640]{1,0:T(8,128)(2,1)S(1)}, bf16[64,640]{1,0:T(8,128)(2,1)S(1)}, u32[]{:S(2)}, u32[]{:S(2)}) collective-permute-start(bf16[64,640]{1,0:T(8,128)(2,1)S(1)} %get-tuple-element.34), channel_id=1, source_target_pairs={{0,6},{2,4},{4,2},{6,0},{1,7},{3,5},{5,3},{7,1},{8,14},{10,12},{12... | collective-permute-start | bytes 245768 | tf_op jit(solution)/shard_map/ppermute | solution.py:261
  37.3 2.0 %collective-permute-start.11 = (f32[32,4096]{1,0:T(8,128)S(1)}, f32[32,4096]{1,0:T(8,128)S(1)}, u32[]{:S(2)}, u32[]{:S(2)}) collective-permute-start(f32[32,4096]{1,0:T(8,128)S(1)} %get-tuple-element.36), channel_id=1, source_target_pairs={{0,1},{1,0},{2,3},{3,2},{4,5},{5,4},{6,7},{7,6},{8,9},{9,8},{10,11... | collective-permute-start | bytes 1572872 | tf_op jit(solution)/shard_map/ppermute | solution.py:261
  39.3 4.5 %collective-permute-start.12 = (bf16[8,4096]{1,0:T(8,128)(2,1)S(1)}, bf16[8,4096]{1,0:T(8,128)(2,1)S(1)}, u32[]{:S(2)}, u32[]{:S(2)}) collective-permute-start(bf16[8,4096]{1,0:T(8,128)(2,1)S(1)} %get-tuple-element.38), channel_id=1, source_target_pairs={{0,2},{2,0},{4,6},{6,4},{1,3},{3,1},{5,7},{7,5},{8,10},{10,8},{12,... | collective-permute-start | bytes 196616 | tf_op jit(solution)/shard_map/ppermute | solution.py:261
  40.9 8.2 %collective-permute-start.13 = (bf16[8,4096]{1,0:T(8,128)(2,1)S(1)}, bf16[8,4096]{1,0:T(8,128)(2,1)S(1)}, u32[]{:S(2)}, u32[]{:S(2)}) collective-permute-start(bf16[8,4096]{1,0:T(8,128)(2,1)S(1)} %get-tuple-element.39), channel_id=1, source_target_pairs={{0,4},{2,6},{4,0},{6,2},{1,5},{3,7},{5,1},{7,3},{8,12},{10,14},{12... | collective-permute-start | bytes 196616 | tf_op jit(solution)/shard_map/ppermute | solution.py:261
  42.1 7.0 %collective-permute-start.14 = (bf16[8,4096]{1,0:T(8,128)(2,1)S(1)}, bf16[8,4096]{1,0:T(8,128)(2,1)S(1)}, u32[]{:S(2)}, u32[]{:S(2)}) collective-permute-start(bf16[8,4096]{1,0:T(8,128)(2,1)S(1)} %get-tuple-element.40), channel_id=1, source_target_pairs={{0,6},{2,4},{4,2},{6,0},{1,7},{3,5},{5,3},{7,1},{8,14},{10,12},{12... | collective-permute-start | bytes 196616 | tf_op jit(solution)/shard_map/ppermute | solution.py:261
  49.9 8.6 %collective-permute-start.17 = (bf16[8,4224]{1,0:T(8,128)(2,1)S(1)}, bf16[8,4224]{1,0:T(8,128)(2,1)S(1)}, u32[]{:S(2)}, u32[]{:S(2)}) collective-permute-start(bf16[8,4224]{1,0:T(8,128)(2,1)S(1)} %get-tuple-element.43), channel_id=1, source_target_pairs={{0,6},{2,4},{4,2},{6,0},{1,7},{3,5},{5,3},{7,1},{8,14},{10,12},{12... | collective-permute-start | bytes 202760 | tf_op jit(solution)/shard_map/ppermute | solution.py:261
  52.0 6.5 %collective-permute-start.16 = (bf16[8,4224]{1,0:T(8,128)(2,1)S(1)}, bf16[8,4224]{1,0:T(8,128)(2,1)S(1)}, u32[]{:S(2)}, u32[]{:S(2)}) collective-permute-start(bf16[8,4224]{1,0:T(8,128)(2,1)S(1)} %get-tuple-element.43), channel_id=1, source_target_pairs={{0,4},{2,6},{4,0},{6,2},{1,5},{3,7},{5,1},{7,3},{8,12},{10,14},{12... | collective-permute-start | bytes 202760 | tf_op jit(solution)/shard_map/ppermute | solution.py:261
  52.6 4.7 %collective-permute-start.15 = (bf16[8,4224]{1,0:T(8,128)(2,1)S(1)}, bf16[8,4224]{1,0:T(8,128)(2,1)S(1)}, u32[]{:S(2)}, u32[]{:S(2)}) collective-permute-start(bf16[8,4224]{1,0:T(8,128)(2,1)S(1)} %get-tuple-element.43), channel_id=1, source_target_pairs={{0,2},{2,0},{4,6},{6,4},{1,3},{3,1},{5,7},{7,5},{8,10},{10,8},{12,... | collective-permute-start | bytes 202760 | tf_op jit(solution)/shard_map/ppermute | solution.py:261
  58.5 10.4 %collective-permute-start.20 = (bf16[32,4224]{1,0:T(8,128)(2,1)S(1)}, bf16[32,4224]{1,0:T(8,128)(2,1)S(1)}, u32[]{:S(2)}, u32[]{:S(2)}) collective-permute-start(bf16[32,4224]{1,0:T(8,128)(2,1)S(1)} %constant_dynamic-update-slice_fusion.refs_0_), channel_id=1, source_target_pairs={{0,24},{8,16},{16,8},{24,0},{1,25},{9,17},{17,9},{25,1},{2,26},{10... | collective-permute-start | bytes 811016 | tf_op jit(solution)/shard_map/ppermute | solution.py:261
  61.0 11.7 %collective-permute-start.19 = (bf16[32,4224]{1,0:T(8,128)(2,1)S(1)}, bf16[32,4224]{1,0:T(8,128)(2,1)S(1)}, u32[]{:S(2)}, u32[]{:S(2)}) collective-permute-start(bf16[32,4224]{1,0:T(8,128)(2,1)S(1)} %constant_dynamic-update-slice_fusion.refs_0_), channel_id=1, source_target_pairs={{0,16},{8,24},{16,0},{24,8},{1,17},{9,25},{17,1},{25,9},{2,18},{10... | collective-permute-start | bytes 811016 | tf_op jit(solution)/shard_map/ppermute | solution.py:261
  61.5 11.3 %collective-permute-start.18 = (bf16[32,4224]{1,0:T(8,128)(2,1)S(1)}, bf16[32,4224]{1,0:T(8,128)(2,1)S(1)}, u32[]{:S(2)}, u32[]{:S(2)}) collective-permute-start(bf16[32,4224]{1,0:T(8,128)(2,1)S(1)} %constant_dynamic-update-slice_fusion.refs_0_), channel_id=1, source_target_pairs={{0,8},{8,0},{16,24},{24,16},{1,9},{9,1},{17,25},{25,17},{2,10},{10... | collective-permute-start | bytes 811016 | tf_op jit(solution)/shard_map/ppermute | solution.py:261
  62.1 11.2 %collective-permute-start.21 = (bf16[32,4224]{1,0:T(8,128)(2,1)S(1)}, bf16[32,4224]{1,0:T(8,128)(2,1)S(1)}, u32[]{:S(2)}, u32[]{:S(2)}) collective-permute-start(bf16[32,4224]{1,0:T(8,128)(2,1)S(1)} %constant_dynamic-update-slice_fusion.refs_0_), channel_id=1, source_target_pairs={{0,1},{1,0},{2,3},{3,2},{4,5},{5,4},{6,7},{7,6},{8,9},{9,8},{10,11... | collective-permute-start | bytes 811016 | tf_op jit(solution)/shard_map/ppermute | solution.py:261
  68.9 4.4 %collective-permute-start.24 = (bf16[32,4224]{1,0:T(8,128)(2,1)S(1)}, bf16[32,4224]{1,0:T(8,128)(2,1)S(1)}, u32[]{:S(2)}, u32[]{:S(2)}) collective-permute-start(bf16[32,4224]{1,0:T(8,128)(2,1)S(1)} %collective-permute-done.20.refs_3_), channel_id=1, source_target_pairs={{0,1},{1,0},{2,3},{3,2},{4,5},{5,4},{6,7},{7,6},{8,9},{9,8},{10,11... | collective-permute-start | bytes 811016 | tf_op jit(solution)/shard_map/ppermute | solution.py:261
  72.8 1.8 %collective-permute-start.22 = (bf16[32,4224]{1,0:T(8,128)(2,1)S(1)}, bf16[32,4224]{1,0:T(8,128)(2,1)S(1)}, u32[]{:S(2)}, u32[]{:S(2)}) collective-permute-start(bf16[32,4224]{1,0:T(8,128)(2,1)S(1)} %collective-permute-done.18.refs_1_), channel_id=1, source_target_pairs={{0,1},{1,0},{2,3},{3,2},{4,5},{5,4},{6,7},{7,6},{8,9},{9,8},{10,11... | collective-permute-start | bytes 811016 | tf_op jit(solution)/shard_map/ppermute | solution.py:261
  80.4 1.6 %collective-permute-start.26 = (bf16[32,4096]{1,0:T(8,128)(2,1)S(1)}, bf16[32,4096]{1,0:T(8,128)(2,1)S(1)}, u32[]{:S(2)}, u32[]{:S(2)}) collective-permute-start(bf16[32,4096]{1,0:T(8,128)(2,1)S(1)} %get-tuple-element.47), channel_id=1, source_target_pairs={{0,1},{1,0},{2,3},{3,2},{4,5},{5,4},{6,7},{7,6},{8,9},{9,8},{10,11... | collective-permute-start | bytes 786440 | tf_op jit(solution)/shard_map/ppermute | solution.py:261
  80.6 3.0 %collective-permute-start.28 = (bf16[32,4096]{1,0:T(8,128)(2,1)S(1)}, bf16[32,4096]{1,0:T(8,128)(2,1)S(1)}, u32[]{:S(2)}, u32[]{:S(2)}) collective-permute-start(bf16[32,4096]{1,0:T(8,128)(2,1)S(1)} %get-tuple-element.49), channel_id=1, source_target_pairs={{0,1},{1,0},{2,3},{3,2},{4,5},{5,4},{6,7},{7,6},{8,9},{9,8},{10,11... | collective-permute-start | bytes 786440 | tf_op jit(solution)/shard_map/ppermute | solution.py:261
  80.9 3.6 %collective-permute-start.30 = (bf16[32,4096]{1,0:T(8,128)(2,1)S(1)}, bf16[32,4096]{1,0:T(8,128)(2,1)S(1)}, u32[]{:S(2)}, u32[]{:S(2)}) collective-permute-start(bf16[32,4096]{1,0:T(8,128)(2,1)S(1)} %get-tuple-element.51), channel_id=1, source_target_pairs={{0,1},{1,0},{2,3},{3,2},{4,5},{5,4},{6,7},{7,6},{8,9},{9,8},{10,11... | collective-permute-start | bytes 786440 | tf_op jit(solution)/shard_map/ppermute | solution.py:261
  81.1 4.8 %collective-permute-start.25 = (bf16[32,4096]{1,0:T(8,128)(2,1)S(1)}, bf16[32,4096]{1,0:T(8,128)(2,1)S(1)}, u32[]{:S(2)}, u32[]{:S(2)}) collective-permute-start(bf16[32,4096]{1,0:T(8,128)(2,1)S(1)} %get-tuple-element.45), channel_id=1, source_target_pairs={{0,1},{1,0},{2,3},{3,2},{4,5},{5,4},{6,7},{7,6},{8,9},{9,8},{10,11... | collective-permute-start | bytes 786440 | tf_op jit(solution)/shard_map/ppermute | solution.py:261
  82.0 9.2 %collective-permute-start.27 = (bf16[32,4096]{1,0:T(8,128)(2,1)S(1)}, bf16[32,4096]{1,0:T(8,128)(2,1)S(1)}, u32[]{:S(2)}, u32[]{:S(2)}) collective-permute-start(bf16[32,4096]{1,0:T(8,128)(2,1)S(1)} %add_core.5), channel_id=1, source_target_pairs={{0,8},{8,0},{16,24},{24,16},{1,9},{9,1},{17,25},{25,17},{2,10},{10... | collective-permute-start | bytes 786440 | tf_op jit(solution)/shard_map/ppermute | solution.py:261
  83.7 13.8 %collective-permute-start.29 = (bf16[32,4096]{1,0:T(8,128)(2,1)S(1)}, bf16[32,4096]{1,0:T(8,128)(2,1)S(1)}, u32[]{:S(2)}, u32[]{:S(2)}) collective-permute-start(bf16[32,4096]{1,0:T(8,128)(2,1)S(1)} %add_core.6), channel_id=1, source_target_pairs={{0,16},{8,24},{16,0},{24,8},{1,17},{9,25},{17,1},{25,9},{2,18},{10... | collective-permute-start | bytes 786440 | tf_op jit(solution)/shard_map/ppermute | solution.py:261
  84.6 12.8 %collective-permute-start.31 = (bf16[32,4096]{1,0:T(8,128)(2,1)S(1)}, bf16[32,4096]{1,0:T(8,128)(2,1)S(1)}, u32[]{:S(2)}, u32[]{:S(2)}) collective-permute-start(bf16[32,4096]{1,0:T(8,128)(2,1)S(1)} %add_core.7), channel_id=1, source_target_pairs={{0,24},{8,16},{16,8},{24,0},{1,25},{9,17},{17,9},{25,1},{2,26},{10... | collective-permute-start | bytes 786440 | tf_op jit(solution)/shard_map/ppermute | solution.py:261
  97.5 4.5 %collective-permute-start.32 = (bf16[8,4096]{1,0:T(8,128)(2,1)S(1)}, bf16[8,4096]{1,0:T(8,128)(2,1)S(1)}, u32[]{:S(2)}, u32[]{:S(2)}) collective-permute-start(bf16[8,4096]{1,0:T(8,128)(2,1)S(1)} %get-tuple-element.53), channel_id=1, source_target_pairs={{0,2},{2,0},{4,6},{6,4},{1,3},{3,1},{5,7},{7,5},{8,10},{10,8},{12,... | collective-permute-start | bytes 196616 | tf_op jit(solution)/shard_map/ppermute | solution.py:261
  97.6 5.7 %collective-permute-start.33 = (bf16[8,4096]{1,0:T(8,128)(2,1)S(1)}, bf16[8,4096]{1,0:T(8,128)(2,1)S(1)}, u32[]{:S(2)}, u32[]{:S(2)}) collective-permute-start(bf16[8,4096]{1,0:T(8,128)(2,1)S(1)} %get-tuple-element.54), channel_id=1, source_target_pairs={{0,4},{2,6},{4,0},{6,2},{1,5},{3,7},{5,1},{7,3},{8,12},{10,14},{12... | collective-permute-start | bytes 196616 | tf_op jit(solution)/shard_map/ppermute | solution.py:261
  100.9 6.1 %collective-permute-start.34 = (bf16[8,4096]{1,0:T(8,128)(2,1)S(1)}, bf16[8,4096]{1,0:T(8,128)(2,1)S(1)}, u32[]{:S(2)}, u32[]{:S(2)}) collective-permute-start(bf16[8,4096]{1,0:T(8,128)(2,1)S(1)} %get-tuple-element.55), channel_id=1, source_target_pairs={{0,6},{2,4},{4,2},{6,0},{1,7},{3,5},{5,3},{7,1},{8,14},{10,12},{12... | collective-permute-start | bytes 196616 | tf_op jit(solution)/shard_map/ppermute | solution.py:261
  (14 other events, 173.6 us)
